TPU v7x, 32 devices: a whole 2x2x4 slice. The times are simulated.
32 devices in a mesh: fsdp: 16 (over z, y, x), tp: 2 (over core).
Axes of the slice: x: 2, y: 2, z: 4, core: 2. Of those that a mesh axis runs over, the one named last changes fastest.
Arguments:
- hidden_in: bfloat16 [8192, 2560], P(('fsdp', 'tp')), may hold values from -67 to 67
- seq_ids: int32 [16, 512], P('fsdp'), may hold values from 0 to 1, never falling along the last dimension, each value on 1 to 384 neighbouring positions
- block_ids: int32 [16, 512], P('fsdp'), may hold values from 0 to 3, never falling along the last dimension, each value on 1 to 256 neighbouring positions
- clip_limit: float32 [1], replicated, may hold values from 6 to 12
- cotangent: bfloat16 [8192, 2560], P(('fsdp', 'tp')), may hold values from -6 to 6
- q_down: bfloat16 [2560, 768], P(('fsdp', 'tp')), may hold values from -0.125 to 0.125
- kv_down: bfloat16 [2560, 288], P(('fsdp', 'tp')), may hold values from -0.125 to 0.125
- q_up: bfloat16 [768, 3840], P('fsdp', 'tp'), may hold values from -1 to 1
- kv_up: bfloat16 [256, 5120], P('fsdp', 'tp'), may hold values from -0.375 to 0.375
- out_proj: bfloat16 [2560, 2560], P('fsdp', 'tp'), may hold values from -0.5 to 0.5
- gate_proj: bfloat16 [2560, 6400], P('fsdp', 'tp'), may hold values from -0.125 to 0.125
- up_proj: bfloat16 [2560, 6400], P('fsdp', 'tp'), may hold values from -0.125 to 0.125
- down_proj: bfloat16 [2560, 6400], P('fsdp', 'tp'), may hold values from -0.15625 to 0.15625
- in_gain: bfloat16 [2560], P(('fsdp', 'tp')), may hold values from 0.5 to 1.5
- q_gain: bfloat16 [768], P(('fsdp', 'tp')), may hold values from 0.5 to 1.5
- kv_gain: bfloat16 [256], P(('fsdp', 'tp')), may hold values from 0.5 to 1.5
- post_gain: bfloat16 [2560], P(('fsdp', 'tp')), may hold values from 0.5 to 1.5
Outputs:
- layer_out: bfloat16 [8192, 2560], P(('fsdp', 'tp'))
- input_grad: float32 [8192, 2560], P(('fsdp', 'tp'))
- q_down_grad: float32 [2560, 768], P(('fsdp', 'tp'))
- kv_down_grad: float32 [2560, 288], P(('fsdp', 'tp'))
- q_up_grad: float32 [768, 3840], P('fsdp', 'tp')
- kv_up_grad: float32 [256, 5120], P('fsdp', 'tp')
- out_proj_grad: float32 [2560, 2560], P('fsdp', 'tp')
- gate_proj_grad: float32 [2560, 6400], P('fsdp', 'tp')
- up_proj_grad: float32 [2560, 6400], P('fsdp', 'tp')
- down_proj_grad: float32 [2560, 6400], P('fsdp', 'tp')
- in_gain_grad: float32 [2560], P(('fsdp', 'tp'))
- q_gain_grad: float32 [768], P(('fsdp', 'tp'))
- kv_gain_grad: float32 [256], P(('fsdp', 'tp'))
- post_gain_grad: float32 [2560], P(('fsdp', 'tp'))
- q_up_clipped: bfloat16 [768, 3840], P('fsdp', 'tp')
- kv_up_clipped: bfloat16 [256, 5120], P('fsdp', 'tp')
- maxima: float32 [40], P('tp')
- factors: float32 [40], P('tp')
Inputs may be any that keep to these rules, and one draw needn't show every extreme that they name: `seq_ids`: along each row the ids never fall; each row holds two sequences, each of 128 to 384 tokens. `block_ids`: along each row the ids never fall; a block has 1 to 256 tokens and some block of each row has exactly 256.
All inputs are finite; a program needn't handle non-finite values.
Results may differ from a plain program's by a relative error of at most 0.014.
The roundings to bfloat16 on the way count: a program that leaves them out, or rounds other values in their place, can miss the bound.
Values may be sent and summed in bfloat16 or wider, within the bound.
A program may use at most 320 MiB of HBM per device.

v0:
```python
import functools
import math
import jax
import jax.numpy as jnp
from jax import lax
from jax.sharding import PartitionSpec as P

NOPE = 64
ROPE = 32
VD = 64
KVR = 256
eps = 1e-05
resid_scale = 1.4 / math.sqrt(62.0)
rope_base = 10000.0


def rms_scale(value, gain):
    return value * lax.rsqrt(jnp.mean(value * value, axis=-1, keepdims=True) + eps) * gain


def rotate(value, cosine, sine):
    half = value.shape[-1] // 2
    first = value[..., :half]
    second = value[..., half:]
    return jnp.concatenate(
        [first * cosine - second * sine, second * cosine + first * sine], axis=-1
    )


def angles(seq_row, start, count):
    own_ids = lax.dynamic_slice_in_dim(seq_row, start, count)
    earlier = jnp.sum((seq_row[None, :] < own_ids[:, None]).astype(jnp.int32), axis=1)
    place = (start + jnp.arange(count, dtype=jnp.int32) - earlier).astype(jnp.float32)
    freq = jnp.power(rope_base, -jnp.arange(ROPE // 2, dtype=jnp.float32) * (2.0 / ROPE))
    turn = place[:, None] * freq[None, :]
    return (jnp.cos(turn), jnp.sin(turn))


def contract(left, right, left_dim, right_dim):
    return lax.dot_general(
        left, right, (((left_dim,), (right_dim,)), ((), ())), preferred_element_type=jnp.float32
    )


def attend(items, allowed, score_scale):
    query, key_rows, value_rows = items
    raw = jnp.einsum("hqd,hkd->hqk", query, key_rows, preferred_element_type=jnp.float32)
    masked = jnp.where(allowed[None], raw * score_scale, -1e30)
    top = jnp.max(masked, axis=-1, keepdims=True)
    weights = jnp.exp(masked - top)
    total = jnp.sum(weights, axis=-1, keepdims=True)
    mixed = jnp.einsum(
        "hqk,hkd->hqd",
        (weights / total).astype(jnp.bfloat16),
        value_rows,
        preferred_element_type=jnp.float32,
    )
    return (
        mixed.astype(jnp.bfloat16),
        top[..., 0] + jnp.log(total[..., 0]),
        jnp.max(top[..., 0], axis=-1),
    )


def attend_back(items, allowed, score_scale):
    query, key_rows, value_rows, d_mixed, log_total = items
    raw = jnp.einsum("hqd,hkd->hqk", query, key_rows, preferred_element_type=jnp.float32)
    masked = jnp.where(allowed[None], raw * score_scale, -1e30)
    chance = jnp.exp(masked - log_total[..., None])
    d_values = jnp.einsum(
        "hqk,hqd->hkd", chance.astype(jnp.bfloat16), d_mixed, preferred_element_type=jnp.float32
    )
    d_chance = jnp.einsum("hqd,hkd->hqk", d_mixed, value_rows, preferred_element_type=jnp.float32)
    inner = jnp.sum(chance * d_chance, axis=-1, keepdims=True)
    d_raw = (chance * (d_chance - inner) * score_scale).astype(jnp.bfloat16)
    d_query = jnp.einsum("hqk,hkd->hqd", d_raw, key_rows, preferred_element_type=jnp.float32)
    d_key_rows = jnp.einsum("hqk,hqd->hkd", d_raw, query, preferred_element_type=jnp.float32)
    return (d_query, d_key_rows, d_values)


def shards(
    hidden_in,
    seq_ids,
    block_ids,
    clip_limit,
    cotangent,
    q_down,
    kv_down,
    q_up,
    kv_up,
    out_proj,
    gate_proj,
    up_proj,
    down_proj,
    in_gain,
    q_gain,
    kv_gain,
    post_gain,
):
    tokens_here = hidden_in.shape[0]
    seq_row = seq_ids[0]
    block_row = block_ids[0]
    group = seq_row.shape[0]
    heads = q_up.shape[1] // (NOPE + ROPE)
    stride = math.gcd(heads, 4)
    packs = heads // stride
    score_scale = 1.0 / math.sqrt(NOPE + ROPE)
    first_row = lax.axis_index("tp") * tokens_here
    q_down_full, kv_down_full, in_full, post_full, q_gain_full, kv_gain_full = (
        lax.all_gather(q_down, ("fsdp", "tp"), axis=0, tiled=True),
        lax.all_gather(kv_down, ("fsdp", "tp"), axis=0, tiled=True),
        lax.all_gather(in_gain, ("fsdp", "tp"), axis=0, tiled=True),
        lax.all_gather(post_gain, ("fsdp", "tp"), axis=0, tiled=True),
        lax.all_gather(q_gain, ("fsdp", "tp"), axis=0, tiled=True),
        lax.all_gather(kv_gain, ("fsdp", "tp"), axis=0, tiled=True),
    )
    in_float = in_full.astype(jnp.float32)
    post_float = post_full.astype(jnp.float32)
    q_gain_float = q_gain_full.astype(jnp.float32)
    kv_gain_float = kv_gain_full.astype(jnp.float32)
    q_up_full, kv_up_full, out_full, gate_full, up_full, down_full = (
        lax.all_gather(q_up, "fsdp", axis=0, tiled=True),
        lax.all_gather(kv_up, "fsdp", axis=0, tiled=True),
        lax.all_gather(out_proj, "fsdp", axis=0, tiled=True),
        lax.all_gather(gate_proj, "fsdp", axis=0, tiled=True),
        lax.all_gather(up_proj, "fsdp", axis=0, tiled=True),
        lax.all_gather(down_proj, "fsdp", axis=0, tiled=True),
    )
    x_float = hidden_in.astype(jnp.float32)
    x_normed = rms_scale(x_float, in_float).astype(jnp.bfloat16)
    q_pre = jnp.dot(x_normed, q_down_full, preferred_element_type=jnp.float32)
    c_pre = jnp.dot(x_normed, kv_down_full, preferred_element_type=jnp.float32)
    own_cos, own_sin = angles(seq_row, first_row, tokens_here)
    q_latent = rms_scale(q_pre, q_gain_float).astype(jnp.bfloat16)
    kv_latent = rms_scale(c_pre[:, :KVR], kv_gain_float).astype(jnp.bfloat16)
    key_rot = rotate(c_pre[:, KVR:], own_cos, own_sin).astype(jnp.bfloat16)
    q_lat_all, kv_lat_all, key_rot_all = (
        lax.all_gather(q_latent, "tp", axis=0, tiled=True),
        lax.all_gather(kv_latent, "tp", axis=0, tiled=True),
        lax.all_gather(key_rot, "tp", axis=0, tiled=True),
    )
    all_cos, all_sin = angles(seq_row, 0, group)
    q_full = (
        jnp.dot(q_lat_all, q_up_full, preferred_element_type=jnp.float32)
        .reshape(group, heads, NOPE + ROPE)
        .transpose(1, 0, 2)
    )
    kv_full = (
        jnp.dot(kv_lat_all, kv_up_full, preferred_element_type=jnp.float32)
        .reshape(group, heads, NOPE + VD)
        .transpose(1, 0, 2)
    )
    queries = jnp.concatenate(
        [q_full[:, :, :NOPE], rotate(q_full[:, :, NOPE:], all_cos, all_sin)], axis=-1
    ).astype(jnp.bfloat16)
    key_rows = jnp.concatenate(
        [
            kv_full[:, :, :NOPE].astype(jnp.bfloat16),
            jnp.broadcast_to(key_rot_all[None], (heads, group, ROPE)),
        ],
        axis=-1,
    )
    value_rows = kv_full[:, :, NOPE:].astype(jnp.bfloat16)
    allowed = (seq_row[:, None] == seq_row[None, :]) & (block_row[None, :] <= block_row[:, None])
    query_packs = queries.reshape(packs, stride, group, NOPE + ROPE)
    key_packs = key_rows.reshape(packs, stride, group, NOPE + ROPE)
    value_packs = value_rows.reshape(packs, stride, group, VD)
    mixed, log_total, local_peak = lax.map(
        functools.partial(attend, allowed=allowed, score_scale=score_scale),
        (query_packs, key_packs, value_packs),
    )
    attn = mixed.reshape(heads, group, VD).transpose(1, 0, 2).reshape(group, heads * VD)
    branch_part = contract(attn, out_full, 1, 1)
    branch = lax.psum_scatter(branch_part, "tp", scatter_dimension=0, tiled=True)
    mid = x_float + resid_scale * branch
    mid_normed = rms_scale(mid, post_float).astype(jnp.bfloat16)
    mid_all = lax.all_gather(mid_normed, "tp", axis=0, tiled=True)
    gate = jnp.dot(mid_all, gate_full, preferred_element_type=jnp.float32)
    up_value = jnp.dot(mid_all, up_full, preferred_element_type=jnp.float32)
    sigmoid = jax.nn.sigmoid(gate)
    silu_value = gate * sigmoid
    act = (silu_value * up_value).astype(jnp.bfloat16)
    ffn_part = contract(act, down_full, 1, 1)
    ffn = lax.psum_scatter(
        ffn_part.astype(jnp.bfloat16), "tp", scatter_dimension=0, tiled=True
    ).astype(jnp.float32)
    layer_out = (mid + resid_scale * ffn).astype(jnp.bfloat16)
    peaks = lax.pmax(local_peak.reshape(heads), "fsdp")
    limit = clip_limit[0]
    factors = limit / jnp.maximum(peaks, limit)
    root = jnp.sqrt(factors)
    q_cols = jnp.concatenate(
        [
            jnp.broadcast_to(root[:, None], (heads, NOPE)),
            jnp.broadcast_to(factors[:, None], (heads, ROPE)),
        ],
        axis=1,
    ).reshape(heads * (NOPE + ROPE))
    kv_cols = jnp.concatenate(
        [jnp.broadcast_to(root[:, None], (heads, NOPE)), jnp.ones((heads, VD), jnp.float32)], axis=1
    ).reshape(heads * (NOPE + VD))
    q_clipped = (q_up.astype(jnp.float32) * q_cols[None, :]).astype(jnp.bfloat16)
    kv_clipped = (kv_up.astype(jnp.float32) * kv_cols[None, :]).astype(jnp.bfloat16)
    q_up_back, kv_up_back, out_back, gate_back, up_back, down_back = (
        lax.all_gather(q_up, "fsdp", axis=0, tiled=True),
        lax.all_gather(kv_up, "fsdp", axis=0, tiled=True),
        lax.all_gather(out_proj, "fsdp", axis=0, tiled=True),
        lax.all_gather(gate_proj, "fsdp", axis=0, tiled=True),
        lax.all_gather(up_proj, "fsdp", axis=0, tiled=True),
        lax.all_gather(down_proj, "fsdp", axis=0, tiled=True),
    )
    cot_float = cotangent.astype(jnp.float32)
    d_ffn = (resid_scale * cot_float).astype(jnp.bfloat16)
    d_ffn_all = lax.all_gather(d_ffn, "tp", axis=0, tiled=True)
    down_grad = contract(d_ffn_all, act, 0, 0)
    d_act = jnp.dot(d_ffn_all, down_back, preferred_element_type=jnp.float32)
    d_gate = (d_act * up_value * (sigmoid * (1.0 + gate * (1.0 - sigmoid)))).astype(jnp.bfloat16)
    d_up = (d_act * silu_value).astype(jnp.bfloat16)
    gate_grad = contract(mid_all, d_gate, 0, 0)
    up_grad = contract(mid_all, d_up, 0, 0)
    d_mid_part = contract(d_gate, gate_back, 1, 1) + contract(d_up, up_back, 1, 1)
    d_mid_normed = lax.psum_scatter(d_mid_part, "tp", scatter_dimension=0, tiled=True)
    post_pull = jax.vjp(rms_scale, mid, post_float)[1]
    d_mid_norm, post_grad = post_pull(d_mid_normed)
    d_mid = cot_float + d_mid_norm
    d_branch = (resid_scale * d_mid).astype(jnp.bfloat16)
    d_branch_all = lax.all_gather(d_branch, "tp", axis=0, tiled=True)
    out_grad = contract(d_branch_all, attn, 0, 0)
    d_attn = jnp.dot(d_branch_all, out_back, preferred_element_type=jnp.float32).astype(
        jnp.bfloat16
    )
    d_mixed = d_attn.reshape(group, heads, VD).transpose(1, 0, 2).reshape(packs, stride, group, VD)
    d_query, d_key_rows, d_values = lax.map(
        functools.partial(attend_back, allowed=allowed, score_scale=score_scale),
        (query_packs, key_packs, value_packs, d_mixed, log_total),
    )
    d_query = d_query.reshape(heads, group, NOPE + ROPE)
    d_key_rows = d_key_rows.reshape(heads, group, NOPE + ROPE)
    d_values = d_values.reshape(heads, group, VD)
    d_q_rot = rotate(d_query[:, :, NOPE:], all_cos, -all_sin)
    d_q = (
        jnp.concatenate([d_query[:, :, :NOPE], d_q_rot], axis=-1)
        .transpose(1, 0, 2)
        .reshape(group, heads * (NOPE + ROPE))
        .astype(jnp.bfloat16)
    )
    d_key_rot_part = jnp.sum(d_key_rows[:, :, NOPE:], axis=0)
    d_kv = (
        jnp.concatenate([d_key_rows[:, :, :NOPE], d_values], axis=-1)
        .transpose(1, 0, 2)
        .reshape(group, heads * (NOPE + VD))
        .astype(jnp.bfloat16)
    )
    q_up_grad = contract(q_lat_all, d_q, 0, 0)
    kv_up_grad = contract(kv_lat_all, d_kv, 0, 0)
    d_q_lat_part = contract(d_q, q_up_back, 1, 1)
    d_kv_lat_part = contract(d_kv, kv_up_back, 1, 1)
    d_q_latent, d_kv_latent, d_key_rot = (
        lax.psum_scatter(d_q_lat_part, "tp", scatter_dimension=0, tiled=True),
        lax.psum_scatter(d_kv_lat_part, "tp", scatter_dimension=0, tiled=True),
        lax.psum_scatter(d_key_rot_part, "tp", scatter_dimension=0, tiled=True),
    )
    q_pull = jax.vjp(rms_scale, q_pre, q_gain_float)[1]
    d_q_pre_float, q_gain_grad = q_pull(d_q_latent)
    kv_pull = jax.vjp(rms_scale, c_pre[:, :KVR], kv_gain_float)[1]
    d_c_lat, kv_gain_grad = kv_pull(d_kv_latent)
    d_c_pre = jnp.concatenate([d_c_lat, rotate(d_key_rot, own_cos, -own_sin)], axis=-1).astype(
        jnp.bfloat16
    )
    d_q_pre = d_q_pre_float.astype(jnp.bfloat16)
    q_down_grad = contract(x_normed, d_q_pre, 0, 0)
    kv_down_grad = contract(x_normed, d_c_pre, 0, 0)
    d_x_normed = contract(d_q_pre, q_down_full, 1, 1) + contract(d_c_pre, kv_down_full, 1, 1)
    in_pull = jax.vjp(rms_scale, x_float, in_float)[1]
    d_x_norm, in_grad = in_pull(d_x_normed)
    input_grad = d_mid + d_x_norm
    q_down_out, kv_down_out, in_out, post_out, q_gain_out, kv_gain_out = (
        lax.psum_scatter(q_down_grad, ("fsdp", "tp"), scatter_dimension=0, tiled=True),
        lax.psum_scatter(kv_down_grad, ("fsdp", "tp"), scatter_dimension=0, tiled=True),
        lax.psum_scatter(in_grad, ("fsdp", "tp"), scatter_dimension=0, tiled=True),
        lax.psum_scatter(post_grad, ("fsdp", "tp"), scatter_dimension=0, tiled=True),
        lax.psum_scatter(q_gain_grad, ("fsdp", "tp"), scatter_dimension=0, tiled=True),
        lax.psum_scatter(kv_gain_grad, ("fsdp", "tp"), scatter_dimension=0, tiled=True),
    )
    q_up_out, kv_up_out, out_out, gate_out, up_out, down_out = (
        lax.psum_scatter(q_up_grad, "fsdp", scatter_dimension=0, tiled=True),
        lax.psum_scatter(kv_up_grad, "fsdp", scatter_dimension=0, tiled=True),
        lax.psum_scatter(out_grad, "fsdp", scatter_dimension=0, tiled=True),
        lax.psum_scatter(gate_grad, "fsdp", scatter_dimension=0, tiled=True),
        lax.psum_scatter(up_grad, "fsdp", scatter_dimension=0, tiled=True),
        lax.psum_scatter(down_grad, "fsdp", scatter_dimension=0, tiled=True),
    )
    return (
        layer_out,
        input_grad,
        q_down_out,
        kv_down_out,
        q_up_out,
        kv_up_out,
        out_out,
        gate_out,
        up_out,
        down_out,
        in_out,
        q_gain_out,
        kv_gain_out,
        post_out,
        q_clipped,
        kv_clipped,
        peaks,
        factors,
    )


def solution(mesh):
    placed = (
        P(("fsdp", "tp"), None),
        P("fsdp", None),
        P("fsdp", None),
        P(),
        P(("fsdp", "tp"), None),
        P(("fsdp", "tp"), None),
        P(("fsdp", "tp"), None),
        P("fsdp", "tp"),
        P("fsdp", "tp"),
        P("fsdp", "tp"),
        P("fsdp", "tp"),
        P("fsdp", "tp"),
        P("fsdp", "tp"),
        P(("fsdp", "tp")),
        P(("fsdp", "tp")),
        P(("fsdp", "tp")),
        P(("fsdp", "tp")),
    )
    return jax.shard_map(
        shards,
        mesh=mesh,
        in_specs=placed,
        out_specs=(
            P(("fsdp", "tp"), None),
            P(("fsdp", "tp"), None),
            P(("fsdp", "tp"), None),
            P(("fsdp", "tp"), None),
            P("fsdp", "tp"),
            P("fsdp", "tp"),
            P("fsdp", "tp"),
            P("fsdp", "tp"),
            P("fsdp", "tp"),
            P("fsdp", "tp"),
            P(("fsdp", "tp")),
            P(("fsdp", "tp")),
            P(("fsdp", "tp")),
            P(("fsdp", "tp")),
            P("fsdp", "tp"),
            P("fsdp", "tp"),
            P("tp"),
            P("tp"),
        ),
        check_vma=False,
    )
```

profile of v0, /device:TPU:10, one launch (start us, length us, event | category | flops | bytes accessed | tf_op | source)
XLA Modules:
  0.0 4047.5 jit_solution(4682745554615388410)
XLA Ops:
  14.1 41.7 %all-reduce.10 = (bf16[2560]{0:T(1024)(128)(2,1)S(1)}, bf16[768]{0:T(1024)(128)(2,1)S(1)}, bf16[256]{0:T(256)(128)(2,1)S(1)}, bf16[2560]{0:T(1024)(128)(2,1)S(1)}) all-reduce(bf16[2560]{0:T(1024)(128)(2,1)S(1)} %dynamic-update-slice, bf16[768]{0:T(1024)(128)(2,1)S(1)} %dynamic-update-slice.1, ...), channel_id=1, replica_groups=mesh['fsdp'=16,'tp'=2] {'fsdp','tp'}, use_global_device_ids=true, to_apply=%add.1 | all-reduce | flops 6144 | bytes 24576
  72.9 52.5 %all-gather.18.cloned.1.call-done = bf16[256,2560]{1,0:T(8,128)(2,1)} async-done(((bf16[16,2560]{1,0:T(8,128)(2,1)}), bf16[256,2560]{1,0:T(8,128)(2,1)}) %all-gather.18.cloned.1.call-update) | async-done | bytes 1310736 | tf_op jit(solution)/shard_map/all_gather | solution.py:123
  135.3 54.2 %all-gather.12.cloned.1.call-done = bf16[2560,768]{1,0:T(8,128)(2,1)} async-done(((bf16[80,768]{1,0:T(8,128)(2,1)}), bf16[2560,768]{1,0:T(8,128)(2,1)}) %all-gather.12.cloned.1.call-update) | async-done | bytes 3932176 | tf_op jit(solution)/shard_map/all_gather | solution.py:110
  196.9 60.9 %all-gather.14.cloned.1.call-done = bf16[768,1920]{1,0:T(8,128)(2,1)} async-done(((bf16[48,1920]{1,0:T(8,128)(2,1)}), bf16[768,1920]{1,0:T(8,128)(2,1)}) %all-gather.14.cloned.1.call-update) | async-done | bytes 2949136 | tf_op jit(solution)/shard_map/all_gather | solution.py:122
  263.6 40.1 while.30
  303.7 51.2 %all-gather.20.cloned.1.call-done = bf16[2560,1280]{1,0:T(8,128)(2,1)} async-done(((bf16[160,1280]{1,0:T(8,128)(2,1)}), bf16[2560,1280]{1,0:T(8,128)(2,1)}) %all-gather.20.cloned.1.call-update) | async-done | bytes 6553616 | tf_op jit(solution)/shard_map/all_gather | solution.py:124
  394.6 190.1 %all-gather.24.cloned.1.call-done = bf16[2560,3200]{1,0:T(8,128)(2,1)} async-done(((bf16[160,3200]{1,0:T(8,128)(2,1)}), bf16[2560,3200]{1,0:T(8,128)(2,1)}) %all-gather.24.cloned.1.call-update) | async-done | bytes 16384016 | tf_op jit(solution)/shard_map/all_gather | solution.py:125
  600.4 173.6 %all-gather.26.cloned.1.call-done = bf16[2560,3200]{1,0:T(8,128)(2,1)} async-done(((bf16[160,3200]{1,0:T(8,128)(2,1)}), bf16[2560,3200]{1,0:T(8,128)(2,1)}) %all-gather.26.cloned.1.call-update) | async-done | bytes 16384016 | tf_op jit(solution)/shard_map/all_gather | solution.py:126
  788.9 188.3 %all-gather.28.cloned.1.call-done = bf16[2560,3200]{1,0:T(8,128)(2,1)} async-done(((bf16[160,3200]{1,0:T(8,128)(2,1)}), bf16[2560,3200]{1,0:T(8,128)(2,1)}) %all-gather.28.cloned.1.call-update) | async-done | bytes 16384016 | tf_op jit(solution)/shard_map/all_gather | solution.py:127
  977.2 21.1 multiply_convert_fusion.1
  998.3 16.1 fusion.127
  1071.4 137.5 %while.31 = (s32[]{:T(128)}, f32[5,4,512,96]{2,3,1,0:T(8,128)}, f32[5,4,512,96]{2,3,1,0:T(8,128)}, bf16[5,4,512,64]{2,3,1,0:T(8,128)(2,1)S(1)}, bf16[5,4,512,96]...) while((s32[]{:T(128)}, f32[5,4,512,96]{2,3,1,0:T(8,128)}, ...), condition=%wide.region_17.18_spmd.clone, body=%wide.region_15.17_spmd.clone.sunk | while | flops 887886848 | bytes 51151992 | solution.py:233
  1276.7 18.2 fusion.133
  1294.9 17.7 fusion.134
  1313.0 17.9 fusion.135
  1331.7 31.0 pmax.7
  1370.9 51.4 %all-reduce.9 = (f32[2560]{0:T(1024)S(1)}, f32[768]{0:T(1024)S(1)}, f32[256]{0:T(256)S(1)}, f32[2560]{0:T(1024)S(1)}) all-reduce(f32[2560]{0:T(1024)S(1)} %get-tuple-element.174, f32[768]{0:T(1024)S(1)} %get-tuple-element.176, f32[256]{0:T(256)S(1)} %get-tuple-element.178, ...), channel_id=16, replica_groups=mesh['fsdp'=16,'tp'=2] {'fsdp','tp'}, use_global_device_ids=true, to_apply=%region_34.35.clone | all-reduce | flops 6144 | bytes 49152
  1430.6 17.7 reduce-scatter.33.cloned.1.call-done
  1448.2 155.2 %reduce-scatter.31.cloned.1.call-done = f32[48,1920]{1,0:T(8,128)} async-done(((f32[768,1920]{1,0:T(8,128)}), f32[48,1920]{1,0:T(8,128)}) %reduce-scatter.31.cloned.1.call-update) | async-done | bytes 368656 | tf_op jit(solution)/shard_map/reduce_scatter | solution.py:286
  1603.5 129.2 %reduce-scatter.27.cloned.1.call-done = f32[80,768]{1,0:T(8,128)} async-done(((f32[2560,768]{1,0:T(8,128)}), f32[80,768]{1,0:T(8,128)}) %reduce-scatter.27.cloned.1.call-update) | async-done | bytes 245776 | tf_op jit(solution)/shard_map/reduce_scatter | solution.py:278
  1732.6 279.7 %reduce-scatter.35.cloned.1.call-done = f32[160,1280]{1,0:T(8,128)} async-done(((f32[2560,1280]{1,0:T(8,128)}), f32[160,1280]{1,0:T(8,128)}) %reduce-scatter.35.cloned.1.call-update) | async-done | bytes 819216 | tf_op jit(solution)/shard_map/reduce_scatter | solution.py:288
  2012.3 676.1 %reduce-scatter.37.cloned.1.call-done = f32[160,3200]{1,0:T(8,128)} async-done(((f32[2560,3200]{1,0:T(8,128)}), f32[160,3200]{1,0:T(8,128)}) %reduce-scatter.37.cloned.1.call-update) | async-done | bytes 2048016 | tf_op jit(solution)/shard_map/reduce_scatter | solution.py:289
  2688.5 676.1 %reduce-scatter.39.cloned.1.call-done = f32[160,3200]{1,0:T(8,128)} async-done(((f32[2560,3200]{1,0:T(8,128)}), f32[160,3200]{1,0:T(8,128)}) %reduce-scatter.39.cloned.1.call-update) | async-done | bytes 2048016 | tf_op jit(solution)/shard_map/reduce_scatter | solution.py:290
  3364.6 676.1 %reduce-scatter.41.cloned.1.call-done = f32[160,3200]{1,0:T(8,128)} async-done(((f32[2560,3200]{1,0:T(8,128)}), f32[160,3200]{1,0:T(8,128)}) %reduce-scatter.41.cloned.1.call-update) | async-done | bytes 2048016 | tf_op jit(solution)/shard_map/reduce_scatter | solution.py:291
  (351 shorter events, 435.3 us)
Async XLA Ops:
  7.2 60.1 %all-gather.16.cloned.1.call-start = ((), (), s32[]{:S(2)}) async-start(), calls=%async_computation.16 | async-start | bytes 2027520 | tf_op jit(solution)/shard_map/all_gather | solution.py:111
  7.9 117.5 %all-gather.18.cloned.1.call-start = ((), (), s32[]{:S(2)}) async-start(), calls=%async_computation.17 | async-start | bytes 1392640 | tf_op jit(solution)/shard_map/all_gather | solution.py:123
  8.7 180.8 %all-gather.12.cloned.1.call-start = ((), (), s32[]{:S(2)}) async-start(), calls=%async_computation.14 | async-start | bytes 4055040 | tf_op jit(solution)/shard_map/all_gather | solution.py:110
  9.4 248.5 %all-gather.14.cloned.1.call-start = ((), (), s32[]{:S(2)}) async-start(), calls=%async_computation.15 | async-start | bytes 3133440 | tf_op jit(solution)/shard_map/all_gather | solution.py:122
  10.0 344.9 %all-gather.20.cloned.1.call-start = ((), (), s32[]{:S(2)}) async-start(), calls=%async_computation.18 | async-start | bytes 6963200 | tf_op jit(solution)/shard_map/all_gather | solution.py:124
  10.6 366.2 %reduce-scatter.15.cloned.1.call-start = ((), (), s32[]{:S(2)}) async-start(), calls=%async_computation.19 | async-start | bytes 7864320 | tf_op jit(solution)/shard_map/reduce_scatter | solution.py:174
  364.1 30.5 all-gather.22.cloned.1.call-start
  382.0 202.7 %all-gather.24.cloned.1.call-start = ((), (), s32[]{:S(2)}) async-start(), calls=%async_computation.21 | async-start | bytes 17408000 | tf_op jit(solution)/shard_map/all_gather | solution.py:125
  382.7 391.2 %all-gather.26.cloned.1.call-start = ((), (), s32[]{:S(2)}) async-start(), calls=%async_computation.22 | async-start | bytes 17408000 | tf_op jit(solution)/shard_map/all_gather | solution.py:126
  383.5 405.5 %all-gather.30.cloned.1.call-start = ((), (), s32[]{:S(2)}) async-start(), calls=%async_computation.25 | async-start | bytes 3932160 | tf_op jit(solution)/shard_map/all_gather | solution.py:214
  384.8 592.4 %all-gather.28.cloned.1.call-start = ((), (), s32[]{:S(2)}) async-start(), calls=%async_computation.23 | async-start | bytes 17408000 | tf_op jit(solution)/shard_map/all_gather | solution.py:127
  385.6 657.4 %reduce-scatter.19.cloned.1.call-start = ((), (), s32[]{:S(2)}) async-start(), calls=%async_computation.26 | async-start | bytes 7864320 | tf_op jit(solution)/shard_map/reduce_scatter | solution.py:222
  1029.3 31.8 all-gather.32.cloned.1.call-start
  1048.4 190.1 %reduce-scatter.25.cloned.1.call-start = ((), (), s32[]{:S(2)}) async-start(), calls=%async_computation.30 | async-start | bytes 98304 | tf_op jit(solution)/shard_map/reduce_scatter | solution.py:261
  1216.4 41.2 %reduce-scatter.21.cloned.1.call-start = ((), (), s32[]{:S(2)}) async-start(), calls=%async_computation.28 | async-start | bytes 2359296 | tf_op jit(solution)/shard_map/reduce_scatter | solution.py:259
  1224.5 200.2 %reduce-scatter.17.cloned.1.call-start = ((), (), s32[]{:S(2)}) async-start(), calls=%async_computation.24 | async-start | bytes 3932160 | tf_op jit(solution)/shard_map/reduce_scatter | solution.py:184
  1238.3 192.3 %reduce-scatter.29.cloned.1.call-start = ((), (), s32[]{:S(2)}) async-start(), calls=%async_computation.32 | async-start | bytes 4055040 | tf_op jit(solution)/shard_map/reduce_scatter | solution.py:279
  1244.9 203.4 %reduce-scatter.33.cloned.1.call-start = ((), (), s32[]{:S(2)}) async-start(), calls=%async_computation.34 | async-start | bytes 2785280 | tf_op jit(solution)/shard_map/reduce_scatter | solution.py:287
  1250.1 353.4 %reduce-scatter.31.cloned.1.call-start = ((), (), s32[]{:S(2)}) async-start(), calls=%async_computation.33 | async-start | bytes 6266880 | tf_op jit(solution)/shard_map/reduce_scatter | solution.py:286
  1257.5 475.1 %reduce-scatter.27.cloned.1.call-start = ((), (), s32[]{:S(2)}) async-start(), calls=%async_computation.31 | async-start | bytes 8110080 | tf_op jit(solution)/shard_map/reduce_scatter | solution.py:278
  1265.9 746.4 %reduce-scatter.35.cloned.1.call-start = ((), (), s32[]{:S(2)}) async-start(), calls=%async_computation.35 | async-start | bytes 13926400 | tf_op jit(solution)/shard_map/reduce_scatter | solution.py:288
  1276.4 1412.0 %reduce-scatter.37.cloned.1.call-start = ((), (), s32[]{:S(2)}) async-start(), calls=%async_computation.36 | async-start | bytes 34816000 | tf_op jit(solution)/shard_map/reduce_scatter | solution.py:289
  1294.9 2069.7 %reduce-scatter.39.cloned.1.call-start = ((), (), s32[]{:S(2)}) async-start(), calls=%async_computation.37 | async-start | bytes 34816000 | tf_op jit(solution)/shard_map/reduce_scatter | solution.py:290
  1312.7 2728.0 %reduce-scatter.41.cloned.1.call-start = ((), (), s32[]{:S(2)}) async-start(), calls=%async_computation.38 | async-start | bytes 34816000 | tf_op jit(solution)/shard_map/reduce_scatter | solution.py:291
  (64 other events, 3252.0 us)
Sparse Core Ops, SparseCore 0:
  10.9 56.2 all-gather.15
  70.0 55.3 all-gather.17
  128.3 61.0 all-gather.11
  192.1 65.7 all-gather.13
  260.4 94.4 all-gather.19
  364.2 12.5 reduce-scatter.14
  382.1 12.4 all-gather.21
  397.7 186.9 all-gather.23
  587.8 186.1 all-gather.25
  775.4 11.6 all-gather.29
  790.2 186.9 all-gather.27
  1029.4 13.5 reduce-scatter.18
  1048.5 12.5 all-gather.31
  1224.3 9.1 reduce-scatter.22
  1236.2 10.2 reduce-scatter.20
  1248.6 11.4 reduce-scatter.16
  1266.8 104.8 reduce-scatter.28
  1374.7 73.4 reduce-scatter.32
  1454.8 148.5 reduce-scatter.30
  1610.7 121.9 reduce-scatter.26
  1735.5 276.7 reduce-scatter.34
  2015.3 673.1 reduce-scatter.36
  2691.4 673.1 reduce-scatter.38
  3367.5 673.1 reduce-scatter.40
  (1 shorter events, 8.5 us)
where the time goes:
time: 4050 us
  waiting for transfers between devices  3440 us (85%)
  matrix products  380 us (9%)
  blocking collectives  131 us (3%)
  other arithmetic  44.1 us (1%)
    reduce_scatter x1, waiting for transfers between devices, shards(): lax.psum_scatter(gate_grad, 'fsdp', scatter_dimension=0, tiled=True)  676 us
    reduce_scatter x1, waiting for transfers between devices, shards(): lax.psum_scatter(down_grad, 'fsdp', scatter_dimension=0, tiled=True)  676 us
    reduce_scatter x1, waiting for transfers between devices, shards(): lax.psum_scatter(up_grad, 'fsdp', scatter_dimension=0, tiled=True)  676 us
    reduce_scatter x1, waiting for transfers between devices, shards(): lax.psum_scatter(out_grad, 'fsdp', scatter_dimension=0, tiled=True)  280 us
    all_gather x1, waiting for transfers between devices, shards(): lax.all_gather(gate_proj, 'fsdp', axis=0, tiled=True)  190 us
    all_gather x1, waiting for transfers between devices, shards(): lax.all_gather(down_proj, 'fsdp', axis=0, tiled=True)  188 us
    all_gather x1, waiting for transfers between devices, shards(): lax.all_gather(up_proj, 'fsdp', axis=0, tiled=True)  174 us
    reduce_scatter x1, waiting for transfers between devices, shards(): lax.psum_scatter(q_up_grad, 'fsdp', scatter_dimension=0, tiled=True)  155 us
  transfers between devices with their start and end apart: 25, of which 19 were waited for; matrix products, arithmetic and copies ran while one was open for 6% of the time, Pallas kernels for 0%

commit v1 on v0

--- a/solution.py
+++ b/solution.py
@@ -118,12 +118,31 @@
     post_float = post_full.astype(jnp.float32)
     q_gain_float = q_gain_full.astype(jnp.float32)
     kv_gain_float = kv_gain_full.astype(jnp.float32)
+
+    def scenes_refer(content):
+        all_values, r2, fresh = (lax.axis_size("fsdp"), lax.axis_index("fsdp"), content.shape[0])
+        rack = [(k0, (k0 + 1) % all_values) for k0 in range(all_values)]
+        row_list = [(k0, (k0 - 1) % all_values) for k0 in range(all_values)]
+        y2 = jnp.zeros((*content.shape[:0], all_values * fresh, *content.shape[1:]), content.dtype)
+        y2 = lax.dynamic_update_slice_in_dim(y2, content, r2 * fresh, axis=0)
+        z = all_values // 2
+        after = arr_out = content
+        for t in range(1, z + 1):
+            after = lax.ppermute(after, "fsdp", rack)
+            y2 = lax.dynamic_update_slice_in_dim(y2, after, (r2 - t) % all_values * fresh, axis=0)
+            if t < all_values - z:
+                arr_out = lax.ppermute(arr_out, "fsdp", row_list)
+                y2 = lax.dynamic_update_slice_in_dim(
+                    y2, arr_out, (r2 + t) % all_values * fresh, axis=0
+                )
+        return y2
+
     q_up_full, kv_up_full, out_full, gate_full, up_full, down_full = (
         lax.all_gather(q_up, "fsdp", axis=0, tiled=True),
         lax.all_gather(kv_up, "fsdp", axis=0, tiled=True),
         lax.all_gather(out_proj, "fsdp", axis=0, tiled=True),
         lax.all_gather(gate_proj, "fsdp", axis=0, tiled=True),
-        lax.all_gather(up_proj, "fsdp", axis=0, tiled=True),
+        scenes_refer(up_proj),
         lax.all_gather(down_proj, "fsdp", axis=0, tiled=True),
     )
     x_float = hidden_in.astype(jnp.float32)

time: 4050 us -> 4220 us (1.042)
  waiting for transfers between devices: 3440 us -> 3560 us
    ppermute x0 -> x15, waiting for transfers between devices: none -> 396 us  [the longest x8 358 us: scenes_refer(): after = lax.ppermute(after, 'fsdp', rack)]
    all_gather x1, waiting for transfers between devices: 190 us -> 0.01 us  [shards(): lax.all_gather(gate_proj, 'fsdp', axis=0, tiled=True)]
  transfers between devices with their start and end apart: 25 -> 40, of which waited for: 19 -> 30; matrix products, arithmetic and copies ran while one was open for 6% -> 7% of each run, Pallas kernels for 0% -> 0%
where the time goes in v1:
time: 4220 us
  waiting for transfers between devices  3560 us (84%)
  matrix products  380 us (9%)
  blocking collectives  131 us (3%)
  local copies, waits for them, and re-layouts  66 us (2%)
  other arithmetic  47.1 us (1%)
    reduce_scatter x1, waiting for transfers between devices, shards(): lax.psum_scatter(down_grad, 'fsdp', scatter_dimension=0, tiled=True)  676 us
    reduce_scatter x1, waiting for transfers between devices, shards(): lax.psum_scatter(up_grad, 'fsdp', scatter_dimension=0, tiled=True)  676 us
    reduce_scatter x1, waiting for transfers between devices, shards(): lax.psum_scatter(gate_grad, 'fsdp', scatter_dimension=0, tiled=True)  676 us
    ppermute x8, waiting for transfers between devices, scenes_refer(): after = lax.ppermute(after, 'fsdp', rack)  358 us
    reduce_scatter x1, waiting for transfers between devices, shards(): lax.psum_scatter(out_grad, 'fsdp', scatter_dimension=0, tiled=True)  280 us
    reduce_scatter x1, waiting for transfers between devices, shards(): lax.psum_scatter(q_up_grad, 'fsdp', scatter_dimension=0, tiled=True)  156 us
    all_gather x1, waiting for transfers between devices, shards(): lax.all_gather(down_proj, 'fsdp', axis=0, tiled=True)  151 us
    dot_general x16, matrix products, contract(): lax.dot_general(left, right, (((left_dim,), (right_dim,)), ((), ())), pre...  146 us
  transfers between devices with their start and end apart: 40, of which 30 were waited for; matrix products, arithmetic and copies ran while one was open for 7% of the time, Pallas kernels for 0%

profile of v1, /device:TPU:10, one launch (start us, length us, event | category | flops | bytes accessed | tf_op | source)
XLA Modules:
  0.0 4217.2 jit_solution(1948138934088579117)
XLA Ops:
  16.7 41.8 all-reduce.10
  73.1 52.5 %all-gather.18.cloned.1.call-done = bf16[256,2560]{1,0:T(8,128)(2,1)} async-done(((bf16[16,2560]{1,0:T(8,128)(2,1)}), bf16[256,2560]{1,0:T(8,128)(2,1)}) %all-gather.18.cloned.1.call-update) | async-done | bytes 1310736 | tf_op jit(solution)/shard_map/all_gather | solution.py:142
  135.4 54.2 %all-gather.12.cloned.1.call-done = bf16[2560,768]{1,0:T(8,128)(2,1)} async-done(((bf16[80,768]{1,0:T(8,128)(2,1)}), bf16[2560,768]{1,0:T(8,128)(2,1)}) %all-gather.12.cloned.1.call-update) | async-done | bytes 3932176 | tf_op jit(solution)/shard_map/all_gather | solution.py:110
  196.7 61.3 %all-gather.14.cloned.1.call-done = bf16[768,1920]{1,0:T(8,128)(2,1)} async-done(((bf16[48,1920]{1,0:T(8,128)(2,1)}), bf16[768,1920]{1,0:T(8,128)(2,1)}) %all-gather.14.cloned.1.call-update) | async-done | bytes 2949136 | tf_op jit(solution)/shard_map/all_gather | solution.py:141
  263.8 43.1 %while.30 = (s32[]{:T(128)}, bf16[5,4,512,64]{2,3,1,0:T(8,128)(2,1)}, f32[5,4,512]{2,1,0:T(4,128)}, f32[5,4]{1,0:T(8,128)}, bf16[5,4,512,96]{2,3,1,0:T(8,128)(2,...) while((s32[]{:T(128)}, ...), condition=%wide.region_9.10_spmd.clone, body=%wide.region_5.9_spmd.clone.sunk | while | flops 350091264 | bytes 15014561 | solution.py:187
  306.8 48.3 %all-gather.20.cloned.1.call-done = bf16[2560,1280]{1,0:T(8,128)(2,1)} async-done(((bf16[160,1280]{1,0:T(8,128)(2,1)}), bf16[2560,1280]{1,0:T(8,128)(2,1)}) %all-gather.20.cloned.1.call-update) | async-done | bytes 6553616 | tf_op jit(solution)/shard_map/all_gather | solution.py:143
  387.8 52.0 %collective-permute-done = bf16[160,3200]{1,0:T(8,128)(2,1)S(1)} collective-permute-done((bf16[160,3200]{1,0:T(8,128)(2,1)S(1)}, bf16[160,3200]{1,0:T(8,128)(2,1)S(1)}, u32[]{:S(2)}, u32[]{:S(2)}) %collective-permute-start) | collective-permute-done | bytes 1024032 | tf_op jit(solution)/shard_map/ppermute | solution.py:131
  441.9 66.1 %collective-permute-done.2 = bf16[160,3200]{1,0:T(8,128)(2,1)} collective-permute-done((bf16[160,3200]{1,0:T(8,128)(2,1)S(1)}, bf16[160,3200]{1,0:T(8,128)(2,1)}, u32[]{:S(2)}, u32[]{:S(2)}) %collective-permute-start.2) | collective-permute-done | bytes 1024032 | tf_op jit(solution)/shard_map/ppermute | solution.py:131
  516.6 42.3 %collective-permute-done.4 = bf16[160,3200]{1,0:T(8,128)(2,1)S(1)} collective-permute-done((bf16[160,3200]{1,0:T(8,128)(2,1)}, bf16[160,3200]{1,0:T(8,128)(2,1)S(1)}, u32[]{:S(2)}, u32[]{:S(2)}) %collective-permute-start.4) | collective-permute-done | bytes 1024032 | tf_op jit(solution)/shard_map/ppermute | solution.py:131
  572.7 48.0 %collective-permute-done.6 = bf16[160,3200]{1,0:T(8,128)(2,1)} collective-permute-done((bf16[160,3200]{1,0:T(8,128)(2,1)S(1)}, bf16[160,3200]{1,0:T(8,128)(2,1)}, u32[]{:S(2)}, u32[]{:S(2)}) %collective-permute-start.6) | collective-permute-done | bytes 1024032 | tf_op jit(solution)/shard_map/ppermute | solution.py:131
  647.1 45.5 %collective-permute-done.8 = bf16[160,3200]{1,0:T(8,128)(2,1)S(1)} collective-permute-done((bf16[160,3200]{1,0:T(8,128)(2,1)}, bf16[160,3200]{1,0:T(8,128)(2,1)S(1)}, u32[]{:S(2)}, u32[]{:S(2)}) %collective-permute-start.8) | collective-permute-done | bytes 1024032 | tf_op jit(solution)/shard_map/ppermute | solution.py:131
  710.1 40.5 collective-permute-done.10
  755.7 38.7 collective-permute-done.12
  840.2 151.1 %all-gather.26.cloned.1.call-done = bf16[2560,3200]{1,0:T(8,128)(2,1)} async-done(((bf16[160,3200]{1,0:T(8,128)(2,1)}), bf16[2560,3200]{1,0:T(8,128)(2,1)}) %all-gather.26.cloned.1.call-update) | async-done | bytes 16384016 | tf_op jit(solution)/shard_map/all_gather | solution.py:146
  1042.7 137.7 %all-gather.30.cloned.1.call-done = bf16[2560,3200]{1,0:T(8,128)(2,1)} async-done(((bf16[160,3200]{1,0:T(8,128)(2,1)}), bf16[2560,3200]{1,0:T(8,128)(2,1)}) %all-gather.30.cloned.1.call-update) | async-done | bytes 16384016 | tf_op jit(solution)/shard_map/all_gather | solution.py:228
  1237.2 141.3 %while.31 = (s32[]{:T(128)}, f32[5,4,512,96]{2,3,1,0:T(8,128)}, f32[5,4,512,96]{2,3,1,0:T(8,128)}, bf16[5,4,512,64]{2,3,1,0:T(8,128)(2,1)S(1)}, bf16[5,4,512,96]...) while((s32[]{:T(128)}, f32[5,4,512,96]{2,3,1,0:T(8,128)}, ...), condition=%wide.region_17.18_spmd.clone, body=%wide.region_15.17_spmd.clone.sunk | while | flops 887886848 | bytes 51151992 | solution.py:252
  1501.6 31.1 pmax.7
  1540.9 51.7 %all-reduce.9 = (f32[2560]{0:T(1024)S(1)}, f32[768]{0:T(1024)S(1)}, f32[256]{0:T(256)S(1)}, f32[2560]{0:T(1024)S(1)}) all-reduce(f32[2560]{0:T(1024)S(1)} %get-tuple-element.174, f32[768]{0:T(1024)S(1)} %get-tuple-element.176, f32[256]{0:T(256)S(1)} %get-tuple-element.178, ...), channel_id=16, replica_groups=mesh['fsdp'=16,'tp'=2] {'fsdp','tp'}, use_global_device_ids=true, to_apply=%region_34.35.clone | all-reduce | flops 6144 | bytes 49152
  1617.5 155.9 %reduce-scatter.31.cloned.1.call-done = f32[48,1920]{1,0:T(8,128)} async-done(((f32[768,1920]{1,0:T(8,128)}), f32[48,1920]{1,0:T(8,128)}) %reduce-scatter.31.cloned.1.call-update) | async-done | bytes 368656 | tf_op jit(solution)/shard_map/reduce_scatter | solution.py:305
  1773.4 129.0 %reduce-scatter.27.cloned.1.call-done = f32[80,768]{1,0:T(8,128)} async-done(((f32[2560,768]{1,0:T(8,128)}), f32[80,768]{1,0:T(8,128)}) %reduce-scatter.27.cloned.1.call-update) | async-done | bytes 245776 | tf_op jit(solution)/shard_map/reduce_scatter | solution.py:297
  1902.4 279.7 %reduce-scatter.35.cloned.1.call-done = f32[160,1280]{1,0:T(8,128)} async-done(((f32[2560,1280]{1,0:T(8,128)}), f32[160,1280]{1,0:T(8,128)}) %reduce-scatter.35.cloned.1.call-update) | async-done | bytes 819216 | tf_op jit(solution)/shard_map/reduce_scatter | solution.py:307
  2182.1 676.1 %reduce-scatter.37.cloned.1.call-done = f32[160,3200]{1,0:T(8,128)} async-done(((f32[2560,3200]{1,0:T(8,128)}), f32[160,3200]{1,0:T(8,128)}) %reduce-scatter.37.cloned.1.call-update) | async-done | bytes 2048016 | tf_op jit(solution)/shard_map/reduce_scatter | solution.py:308
  2858.2 676.1 %reduce-scatter.39.cloned.1.call-done = f32[160,3200]{1,0:T(8,128)} async-done(((f32[2560,3200]{1,0:T(8,128)}), f32[160,3200]{1,0:T(8,128)}) %reduce-scatter.39.cloned.1.call-update) | async-done | bytes 2048016 | tf_op jit(solution)/shard_map/reduce_scatter | solution.py:309
  3534.4 676.2 %reduce-scatter.41.cloned.1.call-done = f32[160,3200]{1,0:T(8,128)} async-done(((f32[2560,3200]{1,0:T(8,128)}), f32[160,3200]{1,0:T(8,128)}) %reduce-scatter.41.cloned.1.call-update) | async-done | bytes 2048016 | tf_op jit(solution)/shard_map/reduce_scatter | solution.py:310
  (410 shorter events, 645.2 us)
Async XLA Ops:
  7.9 117.7 %all-gather.18.cloned.1.call-start = ((), (), s32[]{:S(2)}) async-start(), calls=%async_computation.17 | async-start | bytes 1392640 | tf_op jit(solution)/shard_map/all_gather | solution.py:142
  8.7 180.9 %all-gather.12.cloned.1.call-start = ((), (), s32[]{:S(2)}) async-start(), calls=%async_computation.14 | async-start | bytes 4055040 | tf_op jit(solution)/shard_map/all_gather | solution.py:110
  9.4 248.6 %all-gather.14.cloned.1.call-start = ((), (), s32[]{:S(2)}) async-start(), calls=%async_computation.15 | async-start | bytes 3133440 | tf_op jit(solution)/shard_map/all_gather | solution.py:141
  10.0 345.2 %all-gather.20.cloned.1.call-start = ((), (), s32[]{:S(2)}) async-start(), calls=%async_computation.18 | async-start | bytes 6963200 | tf_op jit(solution)/shard_map/all_gather | solution.py:143
  10.6 366.5 %reduce-scatter.15.cloned.1.call-start = ((), (), s32[]{:S(2)}) async-start(), calls=%async_computation.19 | async-start | bytes 7864320 | tf_op jit(solution)/shard_map/reduce_scatter | solution.py:193
  364.4 460.0 %all-gather.22.cloned.1.call-start = ((), (), s32[]{:S(2)}) async-start(), calls=%async_computation.20 | async-start | bytes 3932160 | tf_op jit(solution)/shard_map/all_gather | solution.py:196
  382.2 442.2 %all-gather.24.cloned.1.call-start = ((), (), s32[]{:S(2)}) async-start(), calls=%async_computation.21 | async-start | bytes 17408000 | tf_op jit(solution)/shard_map/all_gather | solution.py:144
  383.0 457.2 %all-gather.28.cloned.1.call-start = ((), (), s32[]{:S(2)}) async-start(), calls=%async_computation.24 | async-start | bytes 3932160 | tf_op jit(solution)/shard_map/all_gather | solution.py:233
  384.3 606.9 %all-gather.26.cloned.1.call-start = ((), (), s32[]{:S(2)}) async-start(), calls=%async_computation.22 | async-start | bytes 17408000 | tf_op jit(solution)/shard_map/all_gather | solution.py:146
  384.9 795.5 %all-gather.30.cloned.1.call-start = ((), (), s32[]{:S(2)}) async-start(), calls=%async_computation.25 | async-start | bytes 17408000 | tf_op jit(solution)/shard_map/all_gather | solution.py:228
  385.7 823.4 %reduce-scatter.19.cloned.1.call-start = ((), (), s32[]{:S(2)}) async-start(), calls=%async_computation.26 | async-start | bytes 7864320 | tf_op jit(solution)/shard_map/reduce_scatter | solution.py:241
  441.4 73.2 %collective-permute-start.3 = (bf16[160,3200]{1,0:T(8,128)(2,1)S(1)}, bf16[160,3200]{1,0:T(8,128)(2,1)}, u32[]{:S(2)}, u32[]{:S(2)}) collective-permute-start(bf16[160,3200]{1,0:T(8,128)(2,1)S(1)} %collective-permute-done.1), channel_id=1, source_target_pairs={{0,30},{2,0},{4,2},{6,4},{8,6},{10,8},{12,10},{14,12},{16,14},{18,... | collective-permute-start | bytes 3072008 | tf_op jit(solution)/shard_map/ppermute | solution.py:134
  568.8 74.8 %collective-permute-start.7 = (bf16[160,3200]{1,0:T(8,128)(2,1)S(1)}, bf16[160,3200]{1,0:T(8,128)(2,1)S(1)}, u32[]{:S(2)}, u32[]{:S(2)}) collective-permute-start(bf16[160,3200]{1,0:T(8,128)(2,1)S(1)} %collective-permute-done.5), channel_id=1, source_target_pairs={{0,30},{2,0},{4,2},{6,4},{8,6},{10,8},{12,10},{14,12},{16,14},{18,... | collective-permute-start | bytes 3072008 | tf_op jit(solution)/shard_map/ppermute | solution.py:134
  620.7 72.0 %collective-permute-start.8 = (bf16[160,3200]{1,0:T(8,128)(2,1)}, bf16[160,3200]{1,0:T(8,128)(2,1)S(1)}, u32[]{:S(2)}, u32[]{:S(2)}) collective-permute-start(bf16[160,3200]{1,0:T(8,128)(2,1)} %collective-permute-done.6), channel_id=1, source_target_pairs={{0,2},{2,4},{4,6},{6,8},{8,10},{10,12},{12,14},{14,16},{16,18},{18... | collective-permute-start | bytes 3072008 | tf_op jit(solution)/shard_map/ppermute | solution.py:131
  1214.5 193.8 %reduce-scatter.25.cloned.1.call-start = ((), (), s32[]{:S(2)}) async-start(), calls=%async_computation.30 | async-start | bytes 98304 | tf_op jit(solution)/shard_map/reduce_scatter | solution.py:280
  1394.2 200.8 %reduce-scatter.17.cloned.1.call-start = ((), (), s32[]{:S(2)}) async-start(), calls=%async_computation.23 | async-start | bytes 3932160 | tf_op jit(solution)/shard_map/reduce_scatter | solution.py:203
  1408.0 192.8 %reduce-scatter.29.cloned.1.call-start = ((), (), s32[]{:S(2)}) async-start(), calls=%async_computation.32 | async-start | bytes 4055040 | tf_op jit(solution)/shard_map/reduce_scatter | solution.py:298
  1414.7 202.8 %reduce-scatter.33.cloned.1.call-start = ((), (), s32[]{:S(2)}) async-start(), calls=%async_computation.34 | async-start | bytes 2785280 | tf_op jit(solution)/shard_map/reduce_scatter | solution.py:306
  1419.9 353.5 %reduce-scatter.31.cloned.1.call-start = ((), (), s32[]{:S(2)}) async-start(), calls=%async_computation.33 | async-start | bytes 6266880 | tf_op jit(solution)/shard_map/reduce_scatter | solution.py:305
  1427.3 475.1 %reduce-scatter.27.cloned.1.call-start = ((), (), s32[]{:S(2)}) async-start(), calls=%async_computation.31 | async-start | bytes 8110080 | tf_op jit(solution)/shard_map/reduce_scatter | solution.py:297
  1435.7 746.4 %reduce-scatter.35.cloned.1.call-start = ((), (), s32[]{:S(2)}) async-start(), calls=%async_computation.35 | async-start | bytes 13926400 | tf_op jit(solution)/shard_map/reduce_scatter | solution.py:307
  1446.2 1412.0 %reduce-scatter.37.cloned.1.call-start = ((), (), s32[]{:S(2)}) async-start(), calls=%async_computation.36 | async-start | bytes 34816000 | tf_op jit(solution)/shard_map/reduce_scatter | solution.py:308
  1464.8 2069.5 %reduce-scatter.39.cloned.1.call-start = ((), (), s32[]{:S(2)}) async-start(), calls=%async_computation.37 | async-start | bytes 34816000 | tf_op jit(solution)/shard_map/reduce_scatter | solution.py:309
  1482.7 2727.9 %reduce-scatter.41.cloned.1.call-start = ((), (), s32[]{:S(2)}) async-start(), calls=%async_computation.38 | async-start | bytes 34816000 | tf_op jit(solution)/shard_map/reduce_scatter | solution.py:310
  (85 other events, 4526.7 us)
Sparse Core Ops, SparseCore 0:
  10.9 56.4 all-gather.15
  70.1 55.4 all-gather.17
  128.5 61.0 all-gather.11
  192.3 65.7 all-gather.13
  260.6 94.5 all-gather.19
  364.5 12.5 reduce-scatter.14
  382.3 12.4 all-gather.21
  397.9 378.7 all-gather.23
  778.3 11.7 all-gather.27
  793.0 198.2 all-gather.25
  994.3 186.1 all-gather.29
  1195.4 13.5 reduce-scatter.18
  1214.6 12.5 all-gather.31
  1394.0 9.1 reduce-scatter.22
  1405.9 10.2 reduce-scatter.20
  1418.3 11.4 reduce-scatter.16
  1436.5 104.6 reduce-scatter.28
  1544.2 73.2 reduce-scatter.32
  1624.0 149.2 reduce-scatter.30
  1780.6 121.7 reduce-scatter.26
  1905.3 276.7 reduce-scatter.34
  2185.0 673.1 reduce-scatter.36
  2861.1 673.1 reduce-scatter.38
  3537.3 673.1 reduce-scatter.40
  (1 shorter events, 8.5 us)
